TPU v7x, 32 devices: a whole 2x2x4 slice. The times are simulated.
32 devices in a mesh: row: 8 (over z, y), leaf: 4 (over x, core).
Axes of the slice: x: 2, y: 2, z: 4, core: 2. Of those that a mesh axis runs over, the one named last changes fastest.
Arguments:
- leaf_index: int32 [8192, 256], P('row', 'leaf'), may hold values from 0 to 63
- targets: float32 [8192, 64], P('row'), may hold values from -6 to 6
Outputs:
- solution: float32 [16384, 64], P('leaf')
- residual: float32 [16384, 64], P('leaf')
All inputs are finite; a program needn't handle non-finite values.
Results may differ from a plain program's by a relative error of at most 0.0003.
Values sent between devices are 32-bit elements; how exact they have to be, the bound alone decides.
No kernel may reach another device: no remote copies, remote signals or barrier semaphores. Data moves between devices by JAX's collectives and lax.ppermute only.
A program may use at most 64 MiB of HBM per device.

v0:
```python
import math
import jax
import jax.numpy as jnp
from jax import lax
from jax.sharding import PartitionSpec as P

LEAVES = 64
ITERS = 2
ridge_weight = 1.0


def indicator(leaf_index, start, count):
    columns = start + jnp.arange(count, dtype=jnp.int32)
    trees = columns // LEAVES
    which = columns % LEAVES
    picked = jnp.take(leaf_index, trees, axis=1)
    return (picked == which[None, :]).astype(jnp.float32)


def forward_local(leaf_index, vector):
    columns = vector.shape[0]
    block_cols = math.gcd(512, columns)

    def step(index, running):
        start = index * block_cols
        marks = indicator(leaf_index, start, block_cols)
        piece = lax.dynamic_slice_in_dim(vector, start, block_cols, 0)
        return running + jnp.dot(
            marks, piece, precision=lax.Precision.HIGHEST, preferred_element_type=jnp.float32
        )

    running = jnp.zeros((leaf_index.shape[0], vector.shape[1]), jnp.float32)
    return lax.fori_loop(0, columns // block_cols, step, running)


def backward_range(leaf_index, values, start, count):
    block_cols = math.gcd(512, count)

    def block(index):
        marks = indicator(leaf_index, start + index * block_cols, block_cols)
        return lax.dot_general(
            marks,
            values,
            (((0,), (0,)), ((), ())),
            precision=lax.Precision.HIGHEST,
            preferred_element_type=jnp.float32,
        )

    blocks = lax.map(block, jnp.arange(count // block_cols, dtype=jnp.int32))
    return blocks.reshape(count, values.shape[1])


def per_device(leaf_index, targets):
    rows_dev = leaf_index.shape[0]
    columns = leaf_index.shape[1] * LEAVES
    scale = (LEAVES / (rows_dev * lax.axis_size("row"))) ** 0.5

    def normal(values):
        local_term = backward_range(leaf_index, values, 0, columns)
        return scale * lax.psum(local_term, "row")

    def total(value):
        return lax.psum(value, "leaf")

    residual = normal(targets)
    solution = jnp.zeros_like(residual)
    direction = residual
    norm_now = total(jnp.sum(residual * residual))
    for step in range(ITERS):
        image = (
            normal(scale * lax.psum(forward_local(leaf_index, direction), "leaf"))
            + ridge_weight * direction
        )
        alpha = norm_now / total(jnp.sum(direction * image))
        solution = solution + alpha * direction
        residual = residual - alpha * image
        norm_next = total(jnp.sum(residual * residual))
        direction = residual + norm_next / norm_now * direction
        norm_now = norm_next
    return (solution, residual)


def solution(mesh):
    return jax.shard_map(
        per_device,
        mesh=mesh,
        in_specs=(P("row", "leaf"), P("row", None)),
        out_specs=(P("leaf", None), P("leaf", None)),
        check_vma=False,
    )
```

profile of v0, /device:TPU:0, one launch (start us, length us, event | category | flops | bytes accessed | tf_op | source)
XLA Modules:
  0.0 664.0 jit_solution(8274413344973260972)
XLA Ops:
  8.3 83.5 %while.68 = (s32[]{:T(128)}, f32[8,512,64]{1,0,2:T(8,128)}, s32[8]{0:T(128)S(1)}, s32[1024,64]{0,1:T(8,128)}, f32[1024,64]{0,1:T(8,128)}, /*index=5*/s32[]{:T(128)}, s32[1]{0:T(128)}, s32[]{:T(128)}) while((s32[]{:T(128)}, f32[8,512,64]{1,0,2:T(8,128)}, s32[8]{0:T(128)S(1)}, s32[1024,64]{0,1:T(8,128)}, f32[1024,64]{0,1:T(8,128)}, ...), condition=%wide.region_1.3_spmd, body=%wide.region_0.2_spmd.sunk | while | flops 403725824 | bytes 8273045 | solution.py:49
  9.7 3.8 gather_fusion
  15.0 3.7 dynamic_update_slice.22
  20.2 3.8 gather_fusion
  25.5 3.7 dynamic_update_slice.22
  30.6 3.8 gather_fusion
  35.9 3.7 dynamic_update_slice.22
  41.0 3.8 gather_fusion
  46.3 3.7 dynamic_update_slice.22
  51.5 3.8 gather_fusion
  56.8 3.7 dynamic_update_slice.22
  61.9 3.8 gather_fusion
  67.2 3.7 dynamic_update_slice.22
  72.4 3.8 gather_fusion
  77.7 3.7 dynamic_update_slice.22
  82.8 3.8 gather_fusion
  88.1 3.7 dynamic_update_slice.22
  91.9 2.8 copy.23
  94.7 81.2 %all-reduce.7.cloned.1.call-done = f32[4096,64]{0,1:T(8,128)} async-done(((f32[4096,64]{0,1:T(8,128)}), f32[4096,64]{0,1:T(8,128)}) %all-reduce.7.cloned.1.call-update) | async-done | bytes 1048592 | tf_op jit(solution)/shard_map/psum | solution.py:60
  178.2 31.5 %while.71 = (s32[]{:T(128)}, f32[1024,64]{0,1:T(8,128)S(1)}, s32[1024,64]{0,1:T(8,128)S(1)}, f32[4096,64]{0,1:T(8,128)}, s32[]{:T(128)}, /*index=5*/s32[]{:T(128)}, s32[]{:T(128)}, s32[]{:T(128)}) while((s32[]{:T(128)}, f32[1024,64]{0,1:T(8,128)S(1)}, s32[1024,64]{0,1:T(8,128)S(1)}, f32[4096,64]{0,1:T(8,128)}, s32[]{:T(128)}, ...), condition=%wide.region_6.8_spmd.clone, body=%wide.region_5.7_spmd.clone.sunk | while | flops 403856896 | bytes 6962329 | solution.py:33
  210.5 32.0 %all-reduce.9.cloned.1.call-done = f32[1024,64]{0,1:T(8,128)} async-done(((f32[1024,64]{0,1:T(8,128)}), f32[1024,64]{0,1:T(8,128)}) %all-reduce.9.cloned.1.call-update) | async-done | bytes 262160 | tf_op jit(solution)/shard_map/psum | solution.py:71
  244.8 68.2 %while.69 = (s32[]{:T(128)}, f32[8,512,64]{1,0,2:T(8,128)}, s32[8]{0:T(128)S(1)}, s32[1024,64]{0,1:T(8,128)S(1)}, f32[1024,64]{1,0:T(8,128)S(1)}, /*index=5*/s32[]{:T(128)}, s32[1]{0:T(128)}, s32[]{:T(128)}) while((s32[]{:T(128)}, f32[8,512,64]{1,0,2:T(8,128)}, s32[8]{0:T(128)S(1)}, s32[1024,64]{0,1:T(8,128)S(1)}, f32[1024,64]{1,0:T(8,128)S(1)}, ...), condition=%wide.region_9.11_spmd, body=%wide.region_8.10_spmd.sunk | while | flops 403725824 | bytes 7224441 | solution.py:49
  249.6 3.7 dynamic_update_slice.23
  258.1 3.7 dynamic_update_slice.23
  266.6 3.7 dynamic_update_slice.23
  275.1 3.7 dynamic_update_slice.23
  283.7 3.7 dynamic_update_slice.23
  292.2 3.7 dynamic_update_slice.23
  300.7 3.7 dynamic_update_slice.23
  309.2 3.7 dynamic_update_slice.23
  313.0 2.9 copy.24
  315.9 78.3 %all-reduce.11.cloned.1.call-done = f32[4096,64]{0,1:T(8,128)} async-done(((f32[4096,64]{0,1:T(8,128)}), f32[4096,64]{0,1:T(8,128)}) %all-reduce.11.cloned.1.call-update) | async-done | bytes 1048592 | tf_op jit(solution)/shard_map/psum | solution.py:60
  396.5 7.1 %all-reduce = (f32[]{:T(128)}, f32[]{:T(128)}) all-reduce(f32[]{:T(128)} %get-tuple-element.487, f32[]{:T(128)} %get-tuple-element.486), channel_id=1, replica_groups=mesh['row'=8,'leaf'=4] {'leaf'}, use_global_device_ids=true, to_apply=%region_4.6 | all-reduce | flops 2 | bytes 16 | tf_op jit(solution)/shard_map/psum | solution.py:63
  405.7 6.3 psum.68
  414.4 37.6 %while.72 = (s32[]{:T(128)}, f32[1024,64]{0,1:T(8,128)}, s32[1024,64]{0,1:T(8,128)S(1)}, f32[4096,64]{0,1:T(8,128)}, s32[]{:T(128)}, /*index=5*/s32[]{:T(128)}, s32[]{:T(128)}, s32[]{:T(128)}) while((s32[]{:T(128)}, f32[1024,64]{0,1:T(8,128)}, s32[1024,64]{0,1:T(8,128)S(1)}, f32[4096,64]{0,1:T(8,128)}, s32[]{:T(128)}, ...), condition=%wide.region_16.18_spmd.clone, body=%wide.region_15.17_spmd.clone.sunk | while | flops 403856896 | bytes 6962329 | solution.py:33
  416.4 2.6 fusion.71
  421.0 2.7 fusion.71
  425.7 2.7 fusion.71
  430.4 2.7 fusion.71
  435.1 2.7 fusion.71
  439.8 2.7 fusion.71
  444.6 2.7 fusion.71
  449.3 2.7 fusion.71
  452.3 31.4 %all-reduce.13.cloned.1.call-done = f32[1024,64]{0,1:T(8,128)} async-done(((f32[1024,64]{0,1:T(8,128)}), f32[1024,64]{0,1:T(8,128)}) %all-reduce.13.cloned.1.call-update) | async-done | bytes 262160 | tf_op jit(solution)/shard_map/psum | solution.py:71
  486.7 75.9 %while.70 = (s32[]{:T(128)}, f32[8,512,64]{1,0,2:T(8,128)}, s32[8]{0:T(128)S(1)}, s32[1024,64]{0,1:T(8,128)S(1)}, f32[1024,64]{1,0:T(8,128)}, /*index=5*/s32[]{:T(128)}, s32[1]{0:T(128)}, s32[]{:T(128)}) while((s32[]{:T(128)}, f32[8,512,64]{1,0,2:T(8,128)}, s32[8]{0:T(128)S(1)}, s32[1024,64]{0,1:T(8,128)S(1)}, f32[1024,64]{1,0:T(8,128)}, ...), condition=%wide.region_19.21_spmd, body=%wide.region_18.20_spmd.sunk | while | flops 403725824 | bytes 7224441 | solution.py:49
  490.0 2.3 fusion.67
  492.5 3.7 dynamic_update_slice.24
  499.5 2.3 fusion.67
  502.0 3.7 dynamic_update_slice.24
  509.0 2.3 fusion.67
  511.5 3.7 dynamic_update_slice.24
  521.0 3.7 dynamic_update_slice.24
  528.0 2.3 fusion.67
  530.4 3.7 dynamic_update_slice.24
  537.5 2.3 fusion.67
  539.9 3.7 dynamic_update_slice.24
  547.0 2.3 fusion.67
  549.4 3.7 dynamic_update_slice.24
  556.5 2.3 fusion.67
  558.9 3.7 dynamic_update_slice.24
  562.7 2.9 copy.25
  565.6 78.5 %all-reduce.15.cloned.1.call-done = f32[4096,64]{0,1:T(8,128)} async-done(((f32[4096,64]{0,1:T(8,128)}), f32[4096,64]{0,1:T(8,128)}) %all-reduce.15.cloned.1.call-update) | async-done | bytes 1048592 | tf_op jit(solution)/shard_map/psum | solution.py:60
  646.2 7.1 %psum.71 = f32[]{:T(128)} all-reduce(f32[]{:T(128)} %multiply_reduce_fusion), channel_id=1, replica_groups=mesh['row'=8,'leaf'=4] {'leaf'}, use_global_device_ids=true, to_apply=%region_22.24 | all-reduce | flops 1 | bytes 8 | tf_op jit(solution)/shard_map/psum | solution.py:63
  654.5 3.0 multiply_subtract_fusion
  (280 shorter events, 136.8 us)
Async XLA Ops:
  7.2 168.8 %all-reduce.7.cloned.1.call-start = ((), (), s32[]{:S(2)}) async-start(), calls=%async_computation | async-start | bytes 2097152 | tf_op jit(solution)/shard_map/psum | solution.py:60
  9.7 3.9 copy-start.6
  20.2 3.9 copy-start.6
  30.6 3.9 copy-start.6
  41.0 3.9 copy-start.6
  51.5 3.9 copy-start.6
  61.9 3.9 copy-start.6
  72.4 3.9 copy-start.6
  82.8 3.9 copy-start.6
  94.7 83.6 %copy-start = (s32[1024,64]{0,1:T(8,128)S(1)}, s32[1024,64]{0,1:T(8,128)}, u32[]{:S(2)}) copy-start(s32[1024,64]{0,1:T(8,128)} %get-tuple-element.836) | copy-start | bytes 786436
  94.7 147.8 %all-reduce.9.cloned.1.call-start = ((), (), s32[]{:S(2)}) async-start(), calls=%async_computation.1 | async-start | bytes 524288 | tf_op jit(solution)/shard_map/psum | solution.py:71
  209.7 0.7 copy-start.5
  210.5 183.8 %all-reduce.11.cloned.1.call-start = ((), (), s32[]{:S(2)}) async-start(), calls=%async_computation.2 | async-start | bytes 2097152 | tf_op jit(solution)/shard_map/psum | solution.py:60
  313.0 81.3 %copy-start.1 = (f32[4096,64]{0,1:T(8,128)S(1)}, f32[4096,64]{0,1:T(8,128)}, u32[]{:S(2)}) copy-start(f32[4096,64]{0,1:T(8,128)} %all-reduce.7.cloned.1.call-done) | copy-start | bytes 3145732
  315.9 167.7 %all-reduce.13.cloned.1.call-start = ((), (), s32[]{:S(2)}) async-start(), calls=%async_computation.3 | async-start | bytes 524288 | tf_op jit(solution)/shard_map/psum | solution.py:71
  394.3 10.6 %copy-start.2 = (f32[4096,64]{0,1:T(8,128)S(1)}, f32[4096,64]{0,1:T(8,128)}, u32[]{:S(2)}) copy-start(f32[4096,64]{0,1:T(8,128)} %all-reduce.11.cloned.1.call-done) | copy-start | bytes 3145732
  452.0 192.0 %all-reduce.15.cloned.1.call-start = ((), (), s32[]{:S(2)}) async-start(), calls=%async_computation.4 | async-start | bytes 2097152 | tf_op jit(solution)/shard_map/psum | solution.py:60
  562.7 81.4 %copy-start.4 = (f32[4096,64]{0,1:T(8,128)S(1)}, f32[4096,64]{0,1:T(8,128)}, u32[]{:S(2)}) copy-start(f32[4096,64]{0,1:T(8,128)} %get-tuple-element.842) | copy-start | bytes 3145732
  565.6 88.9 %copy-start.3 = (f32[4096,64]{0,1:T(8,128)S(1)}, f32[4096,64]{0,1:T(8,128)}, u32[]{:S(2)}) copy-start(f32[4096,64]{0,1:T(8,128)} %all-reduce.11.cloned.1.call-done) | copy-start | bytes 3145732
Sparse Core Ops, SparseCore 0:
  94.8 81.0 all-reduce.6
  210.6 31.8 all-reduce.8
  316.0 78.2 all-reduce.10
  452.2 31.4 all-reduce.12
  565.7 78.3 all-reduce.14
where the time goes:
time: 667 us; the launch traced here: 664 us
  waiting for transfers between devices  301 us (45%)
  local copies, waits for them, and re-layouts  215 us (32%)
  matrix products  76.4 us (11%)
  blocking collectives  20.5 us (3%)
  loops' own time  17.9 us (3%)
  between operations  17.5 us (3%)
  other arithmetic  15.1 us (2%)
    psum x3, waiting for transfers between devices, normal(): return scale * lax.psum(local_term, 'row')  238 us
    dynamic_update_slice x48, local copies, waits for them, and re-layouts, backward_range(): blocks = lax.map(block, jnp.arange(count // block_cols, dtype=jnp.int32))  93.2 us
    gather x40, local copies, waits for them, and re-layouts, indicator(): picked = jnp.take(leaf_index, trees, axis=1)  92 us
    psum x2, waiting for transfers between devices, per_device(): lax.psum(forward_local(leaf_index, direction), 'leaf')  63.3 us
    dot_general x24, matrix products, block(): lax.dot_general(marks, values, (((0,), (0,)), ((), ())), precision=lax.Pr...  39.2 us
    dot_general x16, matrix products, step(): jnp.dot(marks, piece, precision=lax.Precision.HIGHEST, preferred_element_...  37.2 us
    psum x3, blocking collectives, total(): return lax.psum(value, 'leaf')  20.5 us
    another operation x3, loops' own time, backward_range(): blocks = lax.map(block, jnp.arange(count // block_cols, dtype=jnp.int32))  17.2 us
  transfers between devices with their start and end apart: 5, of which 5 were waited for; matrix products, arithmetic and copies ran while one was open for 0% of the time, Pallas kernels for 0%

commit v1 on v0

--- a/solution.py
+++ b/solution.py
@@ -57,7 +57,7 @@
 
     def normal(values):
         local_term = backward_range(leaf_index, values, 0, columns)
-        return scale * lax.psum(local_term, "row")
+        return scale * jnp.sum(lax.all_gather(local_term, "row"), axis=0)
 
     def total(value):
         return lax.psum(value, "leaf")

time: 667 us -> 826 us (1.24)
  waiting for transfers between devices: 301 us -> 437 us
  matrix products: 76.4 us -> 90.7 us
  other arithmetic: 15.1 us -> 25.6 us
    all_gather x0 -> x3, waiting for transfers between devices: none -> 377 us  [normal(): return scale * jnp.sum(lax.all_gather(local_term, 'row'), axis=0)]
    psum x3 -> x0, waiting for transfers between devices: 238 us -> none  [normal(): return scale * lax.psum(local_term, 'row')]
    reduce_sum x0 -> x3, other arithmetic: none -> 12.9 us  [normal(): return scale * jnp.sum(lax.all_gather(local_term, 'row'), axis=0)]
    unnamed x15 -> x8, local copies, waits for them, and re-layouts: 9.3 us -> 0.02 us
    dot_general x24, matrix products: 39.2 us -> 47.5 us  [block(): lax.dot_general(marks, values, (((0,), (0,)), ((), ())), precision=lax.Pr...]
where the time goes in v1:
time: 826 us; the launch traced here: 823 us
  waiting for transfers between devices  437 us (53%)
  local copies, waits for them, and re-layouts  213 us (26%)
  matrix products  90.7 us (11%)
  other arithmetic  25.6 us (3%)
  blocking collectives  20.1 us (2%)
  between operations  18 us (2%)
  loops' own time  17.5 us (2%)
    all_gather x3, waiting for transfers between devices, normal(): return scale * jnp.sum(lax.all_gather(local_term, 'row'), axis=0)  377 us
    dynamic_update_slice x48, local copies, waits for them, and re-layouts, backward_range(): blocks = lax.map(block, jnp.arange(count // block_cols, dtype=jnp.int32))  93.2 us
    gather x40, local copies, waits for them, and re-layouts, indicator(): picked = jnp.take(leaf_index, trees, axis=1)  92 us
    psum x2, waiting for transfers between devices, per_device(): lax.psum(forward_local(leaf_index, direction), 'leaf')  60.5 us
    dot_general x24, matrix products, block(): lax.dot_general(marks, values, (((0,), (0,)), ((), ())), precision=lax.Pr...  47.5 us
    dot_general x16, matrix products, step(): jnp.dot(marks, piece, precision=lax.Precision.HIGHEST, preferred_element_...  43.2 us
    psum x3, blocking collectives, total(): return lax.psum(value, 'leaf')  20.1 us
    another operation x3, loops' own time, backward_range(): blocks = lax.map(block, jnp.arange(count // block_cols, dtype=jnp.int32))  17.1 us
  transfers between devices with their start and end apart: 5, of which 5 were waited for; matrix products, arithmetic and copies ran while one was open for 0% of the time, Pallas kernels for 0%

profile of v1, /device:TPU:0, one launch (start us, length us, event | category | flops | bytes accessed | tf_op | source)
XLA Modules:
  0.0 822.7 jit_solution(8712035144971905334)
XLA Ops:
  8.3 83.5 %while.68 = (s32[]{:T(128)}, f32[8,512,64]{1,0,2:T(8,128)}, s32[8]{0:T(128)S(1)}, s32[1024,64]{0,1:T(8,128)}, f32[1024,64]{0,1:T(8,128)}, /*index=5*/s32[]{:T(128)}, s32[1]{0:T(128)}, s32[]{:T(128)}) while((s32[]{:T(128)}, f32[8,512,64]{1,0,2:T(8,128)}, s32[8]{0:T(128)S(1)}, s32[1024,64]{0,1:T(8,128)}, f32[1024,64]{0,1:T(8,128)}, ...), condition=%wide.region_1.3_spmd, body=%wide.region_0.2_spmd.sunk | while | flops 403725824 | bytes 8273045 | solution.py:49
  9.7 3.8 gather_fusion
  15.0 3.7 dynamic_update_slice.22
  20.2 3.8 gather_fusion
  25.5 3.7 dynamic_update_slice.22
  30.6 3.8 gather_fusion
  35.9 3.7 dynamic_update_slice.22
  41.0 3.8 gather_fusion
  46.3 3.7 dynamic_update_slice.22
  51.5 3.8 gather_fusion
  56.8 3.7 dynamic_update_slice.22
  61.9 3.8 gather_fusion
  67.2 3.7 dynamic_update_slice.22
  72.4 3.8 gather_fusion
  77.7 3.7 dynamic_update_slice.22
  82.8 3.8 gather_fusion
  88.1 3.7 dynamic_update_slice.22
  94.3 127.3 %all-gather.4.cloned.1.call-done = f32[8,4096,64]{1,2,0:T(8,128)} async-done(((f32[1,4096,64]{1,2,0:T(8,128)}), f32[8,4096,64]{1,2,0:T(8,128)}) %all-gather.4.cloned.1.call-update) | async-done | bytes 8388624 | tf_op jit(solution)/shard_map/all_gather | solution.py:60
  221.6 4.0 reduce_sum.63
  226.7 37.5 %while.71 = (s32[]{:T(128)}, f32[1024,64]{0,1:T(8,128)}, s32[1024,64]{0,1:T(8,128)S(1)}, f32[4096,64]{0,1:T(8,128)}, s32[]{:T(128)}, /*index=5*/s32[]{:T(128)}, s32[]{:T(128)}, s32[]{:T(128)}) while((s32[]{:T(128)}, f32[1024,64]{0,1:T(8,128)}, s32[1024,64]{0,1:T(8,128)S(1)}, f32[4096,64]{0,1:T(8,128)}, s32[]{:T(128)}, ...), condition=%wide.region_6.8_spmd.clone, body=%wide.region_5.7_spmd.clone.sunk | while | flops 403856896 | bytes 6962329 | solution.py:33
  228.7 2.6 fusion.69
  233.2 2.7 fusion.69
  237.9 2.7 fusion.69
  242.6 2.7 fusion.69
  247.3 2.7 fusion.69
  252.0 2.7 fusion.69
  256.7 2.7 fusion.69
  261.4 2.7 fusion.69
  264.2 30.6 %all-reduce.4.cloned.1.call-done = f32[1024,64]{0,1:T(8,128)} async-done(((f32[1024,64]{0,1:T(8,128)}), f32[1024,64]{0,1:T(8,128)}) %all-reduce.4.cloned.1.call-update) | async-done | bytes 262160 | tf_op jit(solution)/shard_map/psum | solution.py:71
  297.9 76.5 %while.69 = (s32[]{:T(128)}, f32[8,512,64]{1,0,2:T(8,128)}, s32[8]{0:T(128)S(1)}, s32[1024,64]{0,1:T(8,128)S(1)}, f32[1024,64]{1,0:T(8,128)}, /*index=5*/s32[]{:T(128)}, s32[1]{0:T(128)}, s32[]{:T(128)}) while((s32[]{:T(128)}, f32[8,512,64]{1,0,2:T(8,128)}, s32[8]{0:T(128)S(1)}, s32[1024,64]{0,1:T(8,128)S(1)}, f32[1024,64]{1,0:T(8,128)}, ...), condition=%wide.region_9.11_spmd, body=%wide.region_8.10_spmd.sunk | while | flops 403725824 | bytes 7224441 | solution.py:49
  303.7 3.7 dynamic_update_slice.23
  313.2 3.7 dynamic_update_slice.23
  322.8 3.7 dynamic_update_slice.23
  332.3 3.7 dynamic_update_slice.23
  341.9 3.7 dynamic_update_slice.23
  351.5 3.7 dynamic_update_slice.23
  361.0 3.7 dynamic_update_slice.23
  370.6 3.7 dynamic_update_slice.23
  376.8 124.6 %all-gather.6.cloned.1.call-done = f32[8,4096,64]{1,2,0:T(8,128)} async-done(((f32[1,4096,64]{1,2,0:T(8,128)}), f32[8,4096,64]{1,2,0:T(8,128)}) %all-gather.6.cloned.1.call-update) | async-done | bytes 8388624 | tf_op jit(solution)/shard_map/all_gather | solution.py:60
  501.4 4.0 reduce_sum.65
  506.3 6.5 all-reduce
  515.1 7.1 psum.45
  524.8 37.4 %while.72 = (s32[]{:T(128)}, f32[1024,64]{0,1:T(8,128)}, s32[1024,64]{0,1:T(8,128)S(1)}, f32[4096,64]{0,1:T(8,128)}, s32[]{:T(128)}, /*index=5*/s32[]{:T(128)}, s32[]{:T(128)}, s32[]{:T(128)}) while((s32[]{:T(128)}, f32[1024,64]{0,1:T(8,128)}, s32[1024,64]{0,1:T(8,128)S(1)}, f32[4096,64]{0,1:T(8,128)}, s32[]{:T(128)}, ...), condition=%wide.region_16.18_spmd.clone, body=%wide.region_15.17_spmd.clone.sunk | while | flops 403856896 | bytes 6962329 | solution.py:33
  531.4 2.7 fusion.71
  536.1 2.7 fusion.71
  540.8 2.7 fusion.71
  545.5 2.7 fusion.71
  550.2 2.7 fusion.71
  554.9 2.7 fusion.71
  559.6 2.7 fusion.71
  562.5 29.9 %all-reduce.6.cloned.1.call-done = f32[1024,64]{0,1:T(8,128)} async-done(((f32[1024,64]{0,1:T(8,128)}), f32[1024,64]{0,1:T(8,128)}) %all-reduce.6.cloned.1.call-update) | async-done | bytes 262160 | tf_op jit(solution)/shard_map/psum | solution.py:71
  595.5 75.7 %while.70 = (s32[]{:T(128)}, f32[8,512,64]{1,0,2:T(8,128)}, s32[8]{0:T(128)S(1)}, s32[1024,64]{0,1:T(8,128)S(1)}, f32[1024,64]{1,0:T(8,128)}, /*index=5*/s32[]{:T(128)}, s32[1]{0:T(128)}, s32[]{:T(128)}) while((s32[]{:T(128)}, f32[8,512,64]{1,0,2:T(8,128)}, s32[8]{0:T(128)S(1)}, s32[1024,64]{0,1:T(8,128)S(1)}, f32[1024,64]{1,0:T(8,128)}, ...), condition=%wide.region_19.21_spmd, body=%wide.region_18.20_spmd.sunk | while | flops 403725824 | bytes 7224441 | solution.py:49
  601.2 3.7 dynamic_update_slice.24
  610.7 3.7 dynamic_update_slice.24
  620.1 3.7 dynamic_update_slice.24
  629.6 3.7 dynamic_update_slice.24
  639.1 3.7 dynamic_update_slice.24
  648.5 3.7 dynamic_update_slice.24
  658.0 3.7 dynamic_update_slice.24
  667.4 3.7 dynamic_update_slice.24
  673.6 124.6 %all-gather.8.cloned.1.call-done = f32[8,4096,64]{1,2,0:T(8,128)} async-done(((f32[1,4096,64]{1,2,0:T(8,128)}), f32[8,4096,64]{1,2,0:T(8,128)}) %all-gather.8.cloned.1.call-update) | async-done | bytes 8388624 | tf_op jit(solution)/shard_map/all_gather | solution.py:60
  798.2 4.9 reduce_sum.68
  805.4 6.4 psum.47
  813.2 3.0 multiply_subtract_fusion
  (279 shorter events, 153.3 us)
Async XLA Ops:
  7.2 214.5 %all-gather.4.cloned.1.call-start = ((), (), s32[]{:S(2)}) async-start(), calls=%async_computation | async-start | bytes 9437184 | tf_op jit(solution)/shard_map/all_gather | solution.py:60
  9.7 3.9 copy-start.4
  20.2 3.9 copy-start.4
  30.6 3.9 copy-start.4
  41.0 3.9 copy-start.4
  51.5 3.9 copy-start.4
  61.9 3.9 copy-start.4
  72.4 3.9 copy-start.4
  82.8 3.9 copy-start.4
  94.3 200.5 %all-reduce.4.cloned.1.call-start = ((), (), s32[]{:S(2)}) async-start(), calls=%async_computation.1 | async-start | bytes 524288 | tf_op jit(solution)/shard_map/psum | solution.py:71
  225.6 1.1 copy-start
  264.2 237.2 %all-gather.6.cloned.1.call-start = ((), (), s32[]{:S(2)}) async-start(), calls=%async_computation.2 | async-start | bytes 9437184 | tf_op jit(solution)/shard_map/all_gather | solution.py:60
  376.7 215.7 %all-reduce.6.cloned.1.call-start = ((), (), s32[]{:S(2)}) async-start(), calls=%async_computation.3 | async-start | bytes 524288 | tf_op jit(solution)/shard_map/psum | solution.py:71
  505.3 18.3 %copy-start.1 = (f32[4096,64]{0,1:T(8,128)}, f32[4096,64]{0,1:T(8,128)S(1)}, u32[]{:S(2)}) copy-start(f32[4096,64]{0,1:T(8,128)S(1)} %reduce_sum.65) | copy-start | bytes 3145732
  562.3 236.0 %all-gather.8.cloned.1.call-start = ((), (), s32[]{:S(2)}) async-start(), calls=%async_computation.4 | async-start | bytes 9437184 | tf_op jit(solution)/shard_map/all_gather | solution.py:60
  673.6 129.6 %copy-start.3 = (f32[4096,64]{0,1:T(8,128)S(1)}, f32[4096,64]{0,1:T(8,128)}, u32[]{:S(2)}) copy-start(f32[4096,64]{0,1:T(8,128)} %get-tuple-element.876) | copy-start | bytes 3145732
  803.2 10.0 %copy-start.2 = (f32[4096,64]{0,1:T(8,128)S(1)}, f32[4096,64]{0,1:T(8,128)}, u32[]{:S(2)}) copy-start(f32[4096,64]{0,1:T(8,128)} %copy-done.1) | copy-start | bytes 3145732
Sparse Core Ops, SparseCore 0:
  94.4 127.1 all-gather.3
  264.3 30.4 all-reduce.3
  376.8 124.4 all-gather.5
  562.4 29.9 all-reduce.5
  673.7 124.4 all-gather.7
